TPU v7x, 256 devices: a whole 4x4x8 slice. The times are simulated.
256 devices in a mesh: group: 16 (over z, core), shard: 16 (over y, x).
Axes of the slice: x: 4, y: 4, z: 8, core: 2. Of those that a mesh axis runs over, the one named last changes fastest.
Arguments:
- tokens: bfloat16 [512, 1280], P(('group', 'shard')), as said below
- kv_cache: bfloat16 [512, 128, 2560], P(('group', 'shard'))
- keep_list: int32 [512, 128], P(('group', 'shard')), may hold values from 0 to 1
- lengths: int32 [512], P(('group', 'shard')), may hold values from 64 to 128
- merge_index: int32 [512, 128], P(('group', 'shard')), may hold values from 0 to 15
- merge_table: bfloat16 [16], replicated, may hold values from 0.0099487305 to 0.099609375
- move_offset: int32 [16, 2], P('shard'), may hold values from 0 to 15, as said below
- pair_mask: int32 [16], P('shard'), may hold values from 1 to 15
- w_qkv: bfloat16 [1280, 3840], P(None, 'shard'), may hold values from -0.15625 to 0.15625
- w_out: bfloat16 [1280, 1280], P(None, 'shard'), may hold values from -0.15625 to 0.15625
- w_up: bfloat16 [1280, 5120], P(None, 'shard'), may hold values from -0.15625 to 0.15625
- w_gate: bfloat16 [1280, 5120], P(None, 'shard'), may hold values from -0.15625 to 0.15625
- w_down: bfloat16 [5120, 1280], P('shard'), may hold values from -0.078125 to 0.078125
- qk_scale: float32 [1280], replicated, may hold values from 0.5 to 2
- attn_rate: float32 [1280], replicated, may hold values from 0.05 to 0.5
- mlp_rate: float32 [1280], replicated, may hold values from 0.05 to 0.5
- up_scale: float32 [5120], P('shard'), may hold values from 0.5 to 2
- gate_scale: float32 [5120], P('shard'), may hold values from 0.5 to 2
Outputs:
- new_hidden: bfloat16 [512, 1280], P(('group', 'shard'))
- moved_cache: bfloat16 [512, 128, 2560], P(('group', 'shard'))
Inputs may be any that keep to these rules, and one draw needn't show every extreme that they name: `tokens`: slot 1 of group g and shard s holds the same token as that slot of group g XOR pair_mask[s] on shard s. `move_offset`: the 2 offsets of one shard index are distinct.
All inputs are finite; a program needn't handle non-finite values.
Results may differ from a plain program's by a relative error of at most 0.011.
Values may be sent and summed in bfloat16 or wider, within the bound.
A program may use at most 128 MiB of HBM per device.

v0:
```python
import jax
import jax.numpy as jnp
from jax import lax
from jax.sharding import PartitionSpec as P

DH = 64
BLOCK = 128
WTAB = 16
EPSILON = 1e-06
NEGATIVE = -1e30


def rms_normal(vector):
    return vector * lax.rsqrt(jnp.mean(vector * vector, axis=-1, keepdims=True) + EPSILON)


def head_normal(vector, scaling):
    return vector * lax.rsqrt(jnp.sum(vector * vector, axis=-1, keepdims=True) + EPSILON) * scaling


def rounded(vector):
    return lax.optimization_barrier(vector.astype(jnp.bfloat16)).astype(jnp.float32)


def spread_columns(row_block, weight):
    columns = jnp.dot(
        lax.all_gather(row_block, "shard", axis=0, tiled=True),
        weight,
        preferred_element_type=jnp.float32,
    ).astype(jnp.bfloat16)
    return lax.all_to_all(columns, "shard", split_axis=0, concat_axis=1, tiled=True)


def compact_local(kv_cache, keep_list, lengths, merge_index, merge_table):
    slot_count, context, doubled = kv_cache.shape
    block_count = context // BLOCK
    in_length = jnp.arange(context, dtype=jnp.int32)[None, :] < lengths[:, None]
    keeper = (keep_list == 1) & in_length
    dropper = (keep_list == 0) & in_length
    position = jnp.cumsum(keeper.astype(jnp.int32), axis=1) - 1
    kept_count = jnp.sum(keeper.astype(jnp.int32), axis=1)
    drop_count = jnp.sum(dropper.astype(jnp.int32), axis=1)
    table_hits = merge_index[:, :, None] == jnp.arange(WTAB, dtype=jnp.int32)[None, None, :]
    weights = jnp.sum(
        jnp.where(table_hits, merge_table.astype(jnp.float32)[None, None, :], 0.0), axis=2
    ) * dropper.astype(jnp.float32)
    target = jnp.arange(BLOCK, dtype=jnp.int32)
    placing = (position[:, None, :] == target[None, :, None]) & keeper[:, None, :]
    summing = jnp.where(
        target[None, :, None] == kept_count[:, None, None], weights[:, None, :], 0.0
    )
    mixing = (placing.astype(jnp.float32) + summing).astype(jnp.bfloat16)
    packed = jnp.einsum(
        "ndk,nkc->ndc", mixing, kv_cache, preferred_element_type=jnp.float32
    ).astype(jnp.bfloat16)
    live_count = (kept_count + (drop_count > 0).astype(jnp.int32)).reshape(slot_count, block_count)
    return (packed, live_count.astype(jnp.bfloat16))


def per_device(
    tokens,
    kv_cache,
    keep_list,
    lengths,
    merge_index,
    merge_table,
    move_offset,
    pair_mask,
    w_qkv,
    w_out,
    w_up,
    w_gate,
    w_down,
    qk_scale,
    attn_rate,
    mlp_rate,
    up_scale,
    gate_scale,
):
    slot_count, context, doubled = kv_cache.shape
    model_width = tokens.shape[1]
    head_count = model_width // DH
    group_count = lax.axis_size("group")
    group_index = lax.axis_index("group")
    packed, live_count = compact_local(kv_cache, keep_list, lengths, merge_index, merge_table)
    offsets = move_offset[0]
    target = (group_index + offsets) % group_count
    sender = (jnp.arange(group_count, dtype=jnp.int32)[:, None] == target[None, :]).astype(
        jnp.bfloat16
    )
    outgoing = jnp.einsum("pj,jrc->prc", sender, packed, preferred_element_type=jnp.float32).astype(
        jnp.bfloat16
    )
    outgoing_live = jnp.einsum(
        "pj,jb->pb", sender, live_count, preferred_element_type=jnp.float32
    ).astype(jnp.bfloat16)
    incoming, incoming_live = (
        lax.all_to_all(outgoing, "group", split_axis=0, concat_axis=0, tiled=True),
        lax.all_to_all(outgoing_live, "group", split_axis=0, concat_axis=0, tiled=True),
    )
    source = (group_index - offsets) % group_count
    picker = (source[:, None] == jnp.arange(group_count, dtype=jnp.int32)[None, :]).astype(
        jnp.bfloat16
    )
    moved_cache = jnp.einsum(
        "jp,prc->jrc", picker, incoming, preferred_element_type=jnp.float32
    ).astype(jnp.bfloat16)
    moved_live = jnp.einsum("jp,pb->jb", picker, incoming_live, preferred_element_type=jnp.float32)
    projected = spread_columns(tokens, w_qkv)
    head_scale = qk_scale.reshape(head_count, DH)
    queries = head_normal(
        projected[:, :model_width].astype(jnp.float32).reshape(slot_count, head_count, DH),
        head_scale,
    ).astype(jnp.bfloat16)
    new_keys = head_normal(
        projected[:, model_width : 2 * model_width]
        .astype(jnp.float32)
        .reshape(slot_count, head_count, DH),
        head_scale,
    ).astype(jnp.bfloat16)
    new_values = projected[:, 2 * model_width :].reshape(slot_count, head_count, DH)
    key_rows = moved_cache[:, :, :model_width].reshape(slot_count, context, head_count, DH)
    value_rows = moved_cache[:, :, model_width:].reshape(slot_count, context, head_count, DH)
    score_scale = float(DH) ** 0.5
    scores = score_scale * jnp.einsum(
        "jhd,jrhd->jhr", queries, key_rows, preferred_element_type=jnp.float32
    )
    fresh_score = score_scale * jnp.sum(
        queries.astype(jnp.float32) * new_keys.astype(jnp.float32), axis=-1
    )
    row_valid = (jnp.arange(context, dtype=jnp.int32) % BLOCK).astype(jnp.float32)[
        None, :
    ] < jnp.repeat(moved_live, BLOCK, axis=1)
    pair_bits = pair_mask[0]
    partner = jnp.bitwise_xor(group_index, pair_bits)
    with_new = (jnp.arange(slot_count, dtype=jnp.int32) < slot_count - 1) | (group_index < partner)
    highest = jnp.maximum(
        jnp.max(jnp.where(row_valid[:, None, :], scores, NEGATIVE), axis=2),
        jnp.where(with_new[:, None], fresh_score, NEGATIVE),
    )
    safe_scores = jnp.where(row_valid[:, None, :], scores, highest[:, :, None])
    soft_weights = jnp.where(row_valid[:, None, :], jnp.exp(safe_scores - highest[:, :, None]), 0.0)
    fresh_weight = jnp.where(with_new[:, None], jnp.exp(fresh_score - highest), 0.0)
    weight_sum = jnp.sum(soft_weights, axis=2) + fresh_weight
    weighted = jnp.einsum(
        "jhr,jrhd->jhd",
        soft_weights.astype(jnp.bfloat16),
        value_rows,
        preferred_element_type=jnp.float32,
    )
    weighted = weighted + rounded(fresh_weight)[:, :, None] * new_values.astype(jnp.float32)
    last_high = highest[slot_count - 1 :]
    last_sum = weight_sum[slot_count - 1 :]
    last_weighted = weighted[slot_count - 1 :]
    gathered_high, gathered_sum, gathered_weighted = (
        lax.all_gather(last_high, "group", axis=0, tiled=True),
        lax.all_gather(last_sum, "group", axis=0, tiled=True),
        lax.all_gather(last_weighted, "group", axis=0, tiled=True),
    )
    picker_group = (jnp.arange(group_count, dtype=jnp.int32) == partner).astype(jnp.float32)
    other_high = jnp.sum(picker_group[:, None] * gathered_high, axis=0, keepdims=True)
    other_sum = jnp.sum(picker_group[:, None] * gathered_sum, axis=0, keepdims=True)
    other_weighted = jnp.sum(picker_group[:, None, None] * gathered_weighted, axis=0, keepdims=True)
    merged = jnp.maximum(last_high, other_high)
    own_factor = jnp.exp(last_high - merged)
    other_factor = jnp.exp(other_high - merged)
    long_sum = last_sum * own_factor + other_sum * other_factor
    long_weighted = (
        last_weighted * own_factor[:, :, None] + other_weighted * other_factor[:, :, None]
    )
    weight_sum = jnp.concatenate([weight_sum[: slot_count - 1], long_sum], axis=0)
    weighted = jnp.concatenate([weighted[: slot_count - 1], long_weighted], axis=0)
    attended = (
        (weighted / weight_sum[:, :, None]).reshape(slot_count, model_width).astype(jnp.bfloat16)
    )
    attention_out = spread_columns(attended, w_out)
    hidden = tokens.astype(jnp.float32)
    mixed = rms_normal(
        hidden + attn_rate * (rms_normal(attention_out.astype(jnp.float32)) - hidden)
    )
    mixed_low = mixed.astype(jnp.bfloat16)
    gate_factor = gate_scale * float(model_width) ** 0.5
    shard_rows = lax.all_gather(mixed_low, "shard", axis=0, tiled=True)
    up_part = jnp.dot(shard_rows, w_up, preferred_element_type=jnp.float32) * up_scale
    gate_part = jnp.dot(shard_rows, w_gate, preferred_element_type=jnp.float32) * gate_factor
    inner = (up_part * jax.nn.silu(gate_part)).astype(jnp.bfloat16)
    partial_terms = jnp.dot(inner, w_down, preferred_element_type=jnp.float32)
    mlp_out = lax.psum_scatter(
        partial_terms.astype(jnp.bfloat16), "shard", scatter_dimension=0, tiled=True
    ).astype(jnp.float32)
    new_hidden = rms_normal(mixed + mlp_rate * (rms_normal(mlp_out) - mixed)).astype(jnp.bfloat16)
    return (new_hidden, moved_cache)


def solution(mesh):
    return jax.shard_map(
        per_device,
        mesh=mesh,
        in_specs=(
            P(("group", "shard"), None),
            P(("group", "shard"), None, None),
            P(("group", "shard"), None),
            P(("group", "shard")),
            P(("group", "shard"), None),
            P(),
            P("shard", None),
            P("shard"),
            P(None, "shard"),
            P(None, "shard"),
            P(None, "shard"),
            P(None, "shard"),
            P("shard", None),
            P(),
            P(),
            P(),
            P("shard"),
            P("shard"),
        ),
        out_specs=(P(("group", "shard"), None), P(("group", "shard"), None, None)),
        check_vma=False,
    )
```

profile of v0, /device:TPU:32, one launch (start us, length us, event | category | flops | bytes accessed | tf_op | source)
XLA Modules:
  0.0 549.3 jit_solution(16223864282160331246)
XLA Ops:
  11.9 8.6 %all-to-all-start = ((bf16[16,1,1]{2,1,0:T(2,128)(2,1)}), bf16[16,1,1]{2,1,0:T(2,128)(2,1)S(1)}, u32[]{:S(2)}, u32[]{:S(2)}) async-start(bf16[16,1,1]{2,1,0:T(2,128)(2,1)} %copy.91), calls=%async_computation | async-start | bytes 16384 | tf_op jit(solution)/shard_map/all_to_all | solution.py:99
  20.9 23.9 %all-gather = bf16[16,2,1280]{2,1,0:T(2,128)(2,1)S(1)} all-gather(bf16[1,2,1280]{2,1,0:T(2,128)(2,1)} %bitcast.99), channel_id=1, replica_groups=mesh['group'=16,'shard'=16] {'shard'}, dimensions={0}, use_global_device_ids=true | all-gather | bytes 87040 | tf_op jit(solution)/shard_map/all_gather | solution.py:27
  47.5 4.7 all-to-all-start.1
  52.1 6.1 %convolution_convert_fusion = bf16[16,128,2560]{2,0,1:T(8,128)(2,1)} fusion(bf16[2,128,2560]{2,1,0:T(8,128)(2,1)S(1)} %convolution_convert_fusion.1, s32[2]{0:T(128)S(1)} %fusion.43), kind=kOutput, calls=%fused_computation.2 | convolution fusion | flops 26214432 | bytes 11796488 | tf_op jit(solution)/shard_map/pj,jrc->prc/dot_general | solution.py:91
  58.2 13.7 %copy.94 = bf16[16,128,2560]{2,1,0:T(8,128)(2,1)} copy(bf16[16,128,2560]{2,0,1:T(8,128)(2,1)} %convolution_convert_fusion) | data formatting | bytes 20971520 | tf_op jit(solution)/shard_map/convert_element_type | solution.py:91
  72.0 7.4 %all-to-all-start.2 = ((bf16[16,128,2560]{2,1,0:T(8,128)(2,1)}), bf16[16,128,2560]{2,1,0:T(8,128)(2,1)}, u32[]{:S(2)}, u32[]{:S(2)}) async-start(bf16[16,128,2560]{2,1,0:T(8,128)(2,1)} %copy.94), calls=%async_computation.2 | async-start | bytes 20971520 | tf_op jit(solution)/shard_map/all_to_all | solution.py:98
  81.4 225.6 %all-to-all-done.2 = bf16[16,128,2560]{2,1,0:T(8,128)(2,1)} async-done(((bf16[16,128,2560]{2,1,0:T(8,128)(2,1)}), bf16[16,128,2560]{2,1,0:T(8,128)(2,1)}, u32[]{:S(2)}, u32[]{:S(2)}) %all-to-all-start.2) | async-done | bytes 10485792 | tf_op jit(solution)/shard_map/all_to_all | solution.py:98
  306.9 15.7 %fusion.2 = bf16[2,128,2560]{2,0,1:T(2,128)(2,1)S(1)} fusion(bf16[16,128,2560]{2,1,0:T(8,128)(2,1)} %all-to-all-done.2, s32[2]{0:T(128)S(1)} %and_select_fusion.1), kind=kOutput, calls=%fused_computation.3 | convolution fusion | flops 21626912 | bytes 11796488 | tf_op jit(solution)/shard_map/jp,prc->jrc/dot_general | solution.py:105
  322.7 1.7 fusion.65
  324.4 3.0 copy.96
  327.3 1.4 fusion.25
  329.1 15.7 %all-gather.1 = f32[16,1,20]{2,1,0:T(1,128)S(1)} all-gather(f32[1,1,20]{2,1,0:T(1,128)S(1)} %slice_bitcast_fusion.1), channel_id=1, replica_groups=mesh['group'=16,'shard'=16] {'group'}, dimensions={0}, use_global_device_ids=true | all-gather | bytes 1360 | tf_op jit(solution)/shard_map/all_gather | solution.py:156
  345.1 15.6 %all-gather.2 = f32[16,1,20]{2,1,0:T(1,128)S(1)} all-gather(f32[1,1,20]{2,1,0:T(1,128)S(1)} %slice_bitcast_fusion), channel_id=1, replica_groups=mesh['group'=16,'shard'=16] {'group'}, dimensions={0}, use_global_device_ids=true | all-gather | bytes 1360 | tf_op jit(solution)/shard_map/all_gather | solution.py:157
  361.0 1.9 copy.99
  362.9 1.5 fusion.23
  364.5 15.2 %all_gather.20 = f32[16,20,64]{2,1,0:T(8,128)S(1)} all-gather(f32[1,20,64]{2,1,0:T(8,128)S(1)} %slice.46), channel_id=1, replica_groups=mesh['group'=16,'shard'=16] {'group'}, dimensions={0}, use_global_device_ids=true | all-gather | bytes 87040 | tf_op jit(solution)/shard_map/all_gather | solution.py:158
  380.1 25.8 %all-gather.3 = bf16[16,2,1280]{2,1,0:T(2,128)(2,1)} all-gather(bf16[1,2,1280]{2,1,0:T(2,128)(2,1)S(1)} %fusion.36), channel_id=1, replica_groups=mesh['group'=16,'shard'=16] {'shard'}, dimensions={0}, use_global_device_ids=true | all-gather | bytes 87040 | tf_op jit(solution)/shard_map/all_gather | solution.py:27
  406.8 1.7 convolution_convert_fusion.4
  408.6 4.6 all-to-all-start.3
  413.2 7.4 %all-to-all-done.3 = bf16[16,2,80]{2,1,0:T(2,128)(2,1)S(1)} async-done(((bf16[16,2,80]{2,1,0:T(2,128)(2,1)}), bf16[16,2,80]{2,1,0:T(2,128)(2,1)S(1)}, u32[]{:S(2)}, u32[]{:S(2)}) %all-to-all-start.3) | async-done | bytes 5152 | tf_op jit(solution)/shard_map/all_to_all | solution.py:31
  421.2 23.5 %all-gather.4 = bf16[16,2,1280]{2,1,0:T(2,128)(2,1)} all-gather(bf16[1,2,1280]{2,1,0:T(2,128)(2,1)S(1)} %fusion.35), channel_id=1, replica_groups=mesh['group'=16,'shard'=16] {'shard'}, dimensions={0}, use_global_device_ids=true | all-gather | bytes 87040 | tf_op jit(solution)/shard_map/all_gather | solution.py:183
  445.6 2.1 convolution_multiply_fusion
  447.7 2.6 convolution_convert_fusion.2
  452.7 87.3 %all-reduce.3.cloned.1.call-done = bf16[32,1280]{1,0:T(8,128)(2,1)} async-done(((bf16[32,1280]{1,0:T(8,128)(2,1)}), bf16[32,1280]{1,0:T(8,128)(2,1)}) %all-reduce.3.cloned.1.call-update) | async-done | bytes 81936
  (96 shorter events, 17.1 us)
Async XLA Ops:
  7.2 39.1 %copy-start = (bf16[2,128,2560]{2,1,0:T(8,128)(2,1)S(1)}, bf16[2,128,2560]{2,1,0:T(8,128)(2,1)}, u32[]{:S(2)}) copy-start(bf16[2,128,2560]{2,1,0:T(8,128)(2,1)} %param.19) | copy-start | bytes 3932164
  11.9 35.5 %all-to-all-start = ((bf16[16,1,1]{2,1,0:T(2,128)(2,1)}), bf16[16,1,1]{2,1,0:T(2,128)(2,1)S(1)}, u32[]{:S(2)}, u32[]{:S(2)}) async-start(bf16[16,1,1]{2,1,0:T(2,128)(2,1)} %copy.91), calls=%async_computation | async-start | bytes 16384 | tf_op jit(solution)/shard_map/all_to_all | solution.py:99
  47.5 24.5 %all-to-all-start.1 = ((bf16[16,2,240]{2,1,0:T(2,128)(2,1)}), bf16[16,2,240]{2,1,0:T(2,128)(2,1)S(1)}, u32[]{:S(2)}, u32[]{:S(2)}) async-start(bf16[16,2,240]{2,1,0:T(2,128)(2,1)} %all_to_all.35), calls=%async_computation.1 | async-start | bytes 32768 | tf_op jit(solution)/shard_map/all_to_all | solution.py:31
  72.0 7.4 %copy-start.4 = (f32[1280]{0:T(1024)S(1)}, f32[1280]{0:T(1024)}, u32[]{:S(2)}) copy-start(f32[1280]{0:T(1024)} %param.31) | copy-start | bytes 15364
  72.0 8.1 %copy-start.7 = (s32[1,2]{1,0:T(1,128)S(1)}, s32[1,2]{1,0:T(1,128)}, u32[]{:S(2)}) copy-start(s32[1,2]{1,0:T(1,128)} %param.24) | copy-start | bytes 28
  72.0 235.0 %all-to-all-start.2 = ((bf16[16,128,2560]{2,1,0:T(8,128)(2,1)}), bf16[16,128,2560]{2,1,0:T(8,128)(2,1)}, u32[]{:S(2)}, u32[]{:S(2)}) async-start(bf16[16,128,2560]{2,1,0:T(8,128)(2,1)} %copy.94), calls=%async_computation.2 | async-start | bytes 20971520 | tf_op jit(solution)/shard_map/all_to_all | solution.py:98
  361.0 52.2 %copy-start.6 = (f32[320]{0:T(512)S(1)}, f32[320]{0:T(512)}, u32[]{:S(2)}) copy-start(f32[320]{0:T(512)} %param.35) | copy-start | bytes 3844
  362.9 58.0 %copy-start.2 = (bf16[2,1280]{1,0:T(2,128)(2,1)S(1)}, bf16[2,1280]{1,0:T(2,128)(2,1)}, u32[]{:S(2)}) copy-start(bf16[2,1280]{1,0:T(2,128)(2,1)} %param.18) | copy-start | bytes 15364
  362.9 58.0 %copy-start.3 = (f32[1280]{0:T(1024)S(1)}, f32[1280]{0:T(1024)}, u32[]{:S(2)}) copy-start(f32[1280]{0:T(1024)} %param.32) | copy-start | bytes 15364
  364.4 83.3 %copy-start.1 = (bf16[320,1280]{1,0:T(8,128)(2,1)S(1)}, bf16[320,1280]{1,0:T(8,128)(2,1)}, u32[]{:S(2)}) copy-start(bf16[320,1280]{1,0:T(8,128)(2,1)} %param.30) | copy-start | bytes 2457604
  408.6 12.0 %all-to-all-start.3 = ((bf16[16,2,80]{2,1,0:T(2,128)(2,1)}), bf16[16,2,80]{2,1,0:T(2,128)(2,1)S(1)}, u32[]{:S(2)}, u32[]{:S(2)}) async-start(bf16[16,2,80]{2,1,0:T(2,128)(2,1)} %bitcast.27), calls=%async_computation.3 | async-start | bytes 16384 | tf_op jit(solution)/shard_map/all_to_all | solution.py:31
  413.1 126.9 %all-reduce.3.cloned.1.call-start = ((), (), s32[]{:S(2)}) async-start(), calls=%async_computation.4 | async-start | bytes 163840
  445.6 4.7 copy-start.8
  451.5 89.3 %copy-start.5 = (f32[1280]{0:T(1024)S(1)}, f32[1280]{0:T(1024)}, u32[]{:S(2)}) copy-start(f32[1280]{0:T(1024)} %param.33) | copy-start | bytes 15364
Sparse Core Ops, SparseCore 0:
  450.4 89.5 all-reduce.2
where the time goes:
time: 550 us; the launch traced here: 549 us
  waiting for transfers between devices  320 us (58%)
  blocking collectives  120 us (22%)
  matrix products  33.4 us (6%)
  local copies, waits for them, and re-layouts  26.5 us (5%)
  starting transfers between devices  25.2 us (5%)
  between operations  15.6 us (3%)
  other arithmetic  8.59 us (2%)
    all_to_all x1, waiting for transfers between devices, per_device(): lax.all_to_all(outgoing, 'group', split_axis=0, concat_axis=0, tiled=True)  226 us
    unnamed x2, waiting for transfers between devices  87.3 us
    all_gather x2, blocking collectives, spread_columns(): lax.all_gather(row_block, 'shard', axis=0, tiled=True)  49.7 us
    all_gather x1, blocking collectives, per_device(): shard_rows = lax.all_gather(mixed_low, 'shard', axis=0, tiled=True)  23.5 us
    all_gather x1, blocking collectives, per_device(): lax.all_gather(last_high, 'group', axis=0, tiled=True)  15.7 us
    dot_general x1, matrix products, per_device(): jnp.einsum('jp,prc->jrc', picker, incoming, preferred_element_type=jnp.fl...  15.7 us
    all_gather x1, blocking collectives, per_device(): lax.all_gather(last_sum, 'group', axis=0, tiled=True)  15.6 us
    all_gather x1, blocking collectives, per_device(): lax.all_gather(last_weighted, 'group', axis=0, tiled=True)  15.2 us
  transfers between devices with their start and end apart: 5, of which 3 were waited for; matrix products, arithmetic and copies ran while one was open for 5% of the time, Pallas kernels for 0%

commit v1 on v0

--- a/solution.py
+++ b/solution.py
@@ -180,7 +180,25 @@
     )
     mixed_low = mixed.astype(jnp.bfloat16)
     gate_factor = gate_scale * float(model_width) ** 0.5
-    shard_rows = lax.all_gather(mixed_low, "shard", axis=0, tiled=True)
+
+    def pipes_pack(shard_in):
+        axis_key = "shard"
+        lanes = jax.lax.axis_size(axis_key)
+        outcome_arr = sorted(((q, (q + 1) % lanes) for q in range(lanes)))
+        carry_in = shard_in
+        arrivals = [carry_in]
+        hop_no = 1
+        while hop_no < lanes:
+            carry_in = jax.lax.ppermute(carry_in, axis_key, outcome_arr)
+            arrivals.insert(0, carry_in)
+            hop_no = hop_no + 1
+        return jnp.roll(
+            jnp.concatenate(arrivals, axis=0),
+            (jax.lax.axis_index(axis_key) + 1) * shard_in.shape[0],
+            axis=0,
+        )
+
+    shard_rows = pipes_pack(mixed_low)
     up_part = jnp.dot(shard_rows, w_up, preferred_element_type=jnp.float32) * up_scale
     gate_part = jnp.dot(shard_rows, w_gate, preferred_element_type=jnp.float32) * gate_factor
     inner = (up_part * jax.nn.silu(gate_part)).astype(jnp.bfloat16)

time: 550 us -> 642 us (1.17); the launches traced: 549 us -> 634 us
  waiting for transfers between devices: 320 us -> 413 us
  blocking collectives: 120 us -> 108 us
  local copies, waits for them, and re-layouts: 26.5 us -> 33.9 us
    ppermute x0 -> x15, waiting for transfers between devices: none -> 103 us  [pipes_pack(): carry_in = jax.lax.ppermute(carry_in, axis_key, outcome_arr)]
    all_gather x1 -> x0, blocking collectives: 23.5 us -> none  [per_device(): shard_rows = lax.all_gather(mixed_low, 'shard', axis=0, tiled=True)]
    all_to_all x0 -> x1, blocking collectives: none -> 12 us  [spread_columns(): lax.all_to_all(columns, 'shard', split_axis=0, concat_axis=1, tiled=True)]
    all_to_all x2 -> x1, waiting for transfers between devices: 7.41 us -> 0.01 us  [spread_columns(): lax.all_to_all(columns, 'shard', split_axis=0, concat_axis=1, tiled=True)]
    concatenate x0 -> x1, local copies, waits for them, and re-layouts: none -> 6.66 us  [pipes_pack(): jnp.roll(jnp.concatenate(arrivals, axis=0), (jax.lax.axis_index(axis_key)...]
  transfers between devices with their start and end apart: 5 -> 19, of which waited for: 3 -> 17; matrix products, arithmetic and copies ran while one was open for 5% -> 4% of each run, Pallas kernels for 0% -> 0%
where the time goes in v1:
time: 642 us; the launch traced here: 634 us
  waiting for transfers between devices  413 us (64%)
  blocking collectives  108 us (17%)
  local copies, waits for them, and re-layouts  33.9 us (5%)
  matrix products  32.1 us (5%)
  starting transfers between devices  22 us (3%)
  between operations  15.8 us (2%)
  other arithmetic  9.27 us (1%)
    all_to_all x1, waiting for transfers between devices, per_device(): lax.all_to_all(outgoing, 'group', split_axis=0, concat_axis=0, tiled=True)  225 us
    ppermute x15, waiting for transfers between devices, pipes_pack(): carry_in = jax.lax.ppermute(carry_in, axis_key, outcome_arr)  103 us
    unnamed x2, waiting for transfers between devices  84.9 us
    all_gather x2, blocking collectives, spread_columns(): lax.all_gather(row_block, 'shard', axis=0, tiled=True)  49.7 us
    all_gather x1, blocking collectives, per_device(): lax.all_gather(last_high, 'group', axis=0, tiled=True)  15.7 us
    dot_general x1, matrix products, per_device(): jnp.einsum('jp,prc->jrc', picker, incoming, preferred_element_type=jnp.fl...  15.7 us
    all_gather x1, blocking collectives, per_device(): lax.all_gather(last_sum, 'group', axis=0, tiled=True)  15.6 us
    all_gather x1, blocking collectives, per_device(): lax.all_gather(last_weighted, 'group', axis=0, tiled=True)  15.1 us
  transfers between devices with their start and end apart: 19, of which 17 were waited for; matrix products, arithmetic and copies ran while one was open for 4% of the time, Pallas kernels for 0%

profile of v1, /device:TPU:32, one launch (start us, length us, event | category | flops | bytes accessed | tf_op | source)
XLA Modules:
  0.0 634.4 jit_solution(11099043477280781301)
XLA Ops:
  11.9 8.6 %all-to-all-start = ((bf16[16,1,1]{2,1,0:T(2,128)(2,1)}), bf16[16,1,1]{2,1,0:T(2,128)(2,1)S(1)}, u32[]{:S(2)}, u32[]{:S(2)}) async-start(bf16[16,1,1]{2,1,0:T(2,128)(2,1)} %copy.91), calls=%async_computation | async-start | bytes 16384 | tf_op jit(solution)/shard_map/all_to_all | solution.py:99
  20.9 23.9 %all-gather = bf16[16,2,1280]{2,1,0:T(2,128)(2,1)S(1)} all-gather(bf16[1,2,1280]{2,1,0:T(2,128)(2,1)} %bitcast.96), channel_id=1, replica_groups=mesh['group'=16,'shard'=16] {'shard'}, dimensions={0}, use_global_device_ids=true | all-gather | bytes 87040 | tf_op jit(solution)/shard_map/all_gather | solution.py:27
  58.2 13.7 %copy.94 = bf16[16,128,2560]{2,1,0:T(8,128)(2,1)} copy(bf16[16,128,2560]{2,0,1:T(8,128)(2,1)} %convolution_convert_fusion) | data formatting | bytes 20971520 | tf_op jit(solution)/shard_map/convert_element_type | solution.py:91
  72.0 7.4 %all-to-all-start.2 = ((bf16[16,128,2560]{2,1,0:T(8,128)(2,1)}), bf16[16,128,2560]{2,1,0:T(8,128)(2,1)}, u32[]{:S(2)}, u32[]{:S(2)}) async-start(bf16[16,128,2560]{2,1,0:T(8,128)(2,1)} %copy.94), calls=%async_computation.2 | async-start | bytes 20971520 | tf_op jit(solution)/shard_map/all_to_all | solution.py:98
  81.9 225.1 %all-to-all-done.2 = bf16[16,128,2560]{2,1,0:T(8,128)(2,1)} async-done(((bf16[16,128,2560]{2,1,0:T(8,128)(2,1)}), bf16[16,128,2560]{2,1,0:T(8,128)(2,1)}, u32[]{:S(2)}, u32[]{:S(2)}) %all-to-all-start.2) | async-done | bytes 10485792 | tf_op jit(solution)/shard_map/all_to_all | solution.py:98
  306.9 15.7 %fusion.2 = bf16[2,128,2560]{2,0,1:T(2,128)(2,1)S(1)} fusion(bf16[16,128,2560]{2,1,0:T(8,128)(2,1)} %all-to-all-done.2, s32[2]{0:T(128)S(1)} %and_select_fusion.1), kind=kOutput, calls=%fused_computation.3 | convolution fusion | flops 21626912 | bytes 11796488 | tf_op jit(solution)/shard_map/jp,prc->jrc/dot_general | solution.py:105
  329.0 15.7 %all-gather.1 = f32[16,1,20]{2,1,0:T(1,128)S(1)} all-gather(f32[1,1,20]{2,1,0:T(1,128)S(1)} %slice_bitcast_fusion.1), channel_id=1, replica_groups=mesh['group'=16,'shard'=16] {'group'}, dimensions={0}, use_global_device_ids=true | all-gather | bytes 1360 | tf_op jit(solution)/shard_map/all_gather | solution.py:156
  345.1 15.6 %all-gather.2 = f32[16,1,20]{2,1,0:T(1,128)S(1)} all-gather(f32[1,1,20]{2,1,0:T(1,128)S(1)} %slice_bitcast_fusion), channel_id=1, replica_groups=mesh['group'=16,'shard'=16] {'group'}, dimensions={0}, use_global_device_ids=true | all-gather | bytes 1360 | tf_op jit(solution)/shard_map/all_gather | solution.py:157
  364.5 15.1 %all_gather.17 = f32[16,20,64]{2,1,0:T(8,128)S(1)} all-gather(f32[1,20,64]{2,1,0:T(8,128)S(1)} %slice.46), channel_id=1, replica_groups=mesh['group'=16,'shard'=16] {'group'}, dimensions={0}, use_global_device_ids=true | all-gather | bytes 87040 | tf_op jit(solution)/shard_map/all_gather | solution.py:158
  380.0 25.8 %all-gather.3 = bf16[16,2,1280]{2,1,0:T(2,128)(2,1)} all-gather(bf16[1,2,1280]{2,1,0:T(2,128)(2,1)S(1)} %fusion.38), channel_id=1, replica_groups=mesh['group'=16,'shard'=16] {'shard'}, dimensions={0}, use_global_device_ids=true | all-gather | bytes 87040 | tf_op jit(solution)/shard_map/all_gather | solution.py:27
  407.7 12.0 %all_to_all.46 = bf16[16,2,80]{2,1,0:T(2,128)(2,1)S(1)} all-to-all(bf16[16,2,80]{2,1,0:T(2,128)(2,1)S(1)} %bitcast.93), channel_id=1, replica_groups=mesh['group'=16,'shard'=16] {'shard'}, dimensions={0} | all-to-all | bytes 10240 | tf_op jit(solution)/shard_map/all_to_all | solution.py:31
  427.8 6.9 %collective-permute-done.1 = bf16[2,1280]{1,0:T(2,128)(2,1)S(1)} collective-permute-done((bf16[2,1280]{1,0:T(2,128)(2,1)S(1)}, bf16[2,1280]{1,0:T(2,128)(2,1)S(1)}, u32[]{:S(2)}, u32[]{:S(2)}) %collective-permute-start.1) | collective-permute-done | bytes 5152 | tf_op jit(solution)/shard_map/ppermute | solution.py:192
  434.7 6.9 %collective-permute-done.2 = bf16[2,1280]{1,0:T(2,128)(2,1)S(1)} collective-permute-done((bf16[2,1280]{1,0:T(2,128)(2,1)S(1)}, bf16[2,1280]{1,0:T(2,128)(2,1)S(1)}, u32[]{:S(2)}, u32[]{:S(2)}) %collective-permute-start.2) | collective-permute-done | bytes 5152 | tf_op jit(solution)/shard_map/ppermute | solution.py:192
  441.7 6.9 %collective-permute-done.3 = bf16[2,1280]{1,0:T(2,128)(2,1)S(1)} collective-permute-done((bf16[2,1280]{1,0:T(2,128)(2,1)S(1)}, bf16[2,1280]{1,0:T(2,128)(2,1)S(1)}, u32[]{:S(2)}, u32[]{:S(2)}) %collective-permute-start.3) | collective-permute-done | bytes 5152 | tf_op jit(solution)/shard_map/ppermute | solution.py:192
  448.6 6.9 %collective-permute-done.4 = bf16[2,1280]{1,0:T(2,128)(2,1)S(1)} collective-permute-done((bf16[2,1280]{1,0:T(2,128)(2,1)S(1)}, bf16[2,1280]{1,0:T(2,128)(2,1)S(1)}, u32[]{:S(2)}, u32[]{:S(2)}) %collective-permute-start.4) | collective-permute-done | bytes 5152 | tf_op jit(solution)/shard_map/ppermute | solution.py:192
  455.5 6.9 %collective-permute-done.5 = bf16[2,1280]{1,0:T(2,128)(2,1)S(1)} collective-permute-done((bf16[2,1280]{1,0:T(2,128)(2,1)S(1)}, bf16[2,1280]{1,0:T(2,128)(2,1)S(1)}, u32[]{:S(2)}, u32[]{:S(2)}) %collective-permute-start.5) | collective-permute-done | bytes 5152 | tf_op jit(solution)/shard_map/ppermute | solution.py:192
  462.5 6.9 %collective-permute-done.6 = bf16[2,1280]{1,0:T(2,128)(2,1)S(1)} collective-permute-done((bf16[2,1280]{1,0:T(2,128)(2,1)S(1)}, bf16[2,1280]{1,0:T(2,128)(2,1)S(1)}, u32[]{:S(2)}, u32[]{:S(2)}) %collective-permute-start.6) | collective-permute-done | bytes 5152 | tf_op jit(solution)/shard_map/ppermute | solution.py:192
  469.4 6.9 %collective-permute-done.7 = bf16[2,1280]{1,0:T(2,128)(2,1)S(1)} collective-permute-done((bf16[2,1280]{1,0:T(2,128)(2,1)S(1)}, bf16[2,1280]{1,0:T(2,128)(2,1)S(1)}, u32[]{:S(2)}, u32[]{:S(2)}) %collective-permute-start.7) | collective-permute-done | bytes 5152 | tf_op jit(solution)/shard_map/ppermute | solution.py:192
  476.4 6.9 %collective-permute-done.8 = bf16[2,1280]{1,0:T(2,128)(2,1)S(1)} collective-permute-done((bf16[2,1280]{1,0:T(2,128)(2,1)S(1)}, bf16[2,1280]{1,0:T(2,128)(2,1)S(1)}, u32[]{:S(2)}, u32[]{:S(2)}) %collective-permute-start.8) | collective-permute-done | bytes 5152 | tf_op jit(solution)/shard_map/ppermute | solution.py:192
  483.3 6.9 %collective-permute-done.9 = bf16[2,1280]{1,0:T(2,128)(2,1)S(1)} collective-permute-done((bf16[2,1280]{1,0:T(2,128)(2,1)S(1)}, bf16[2,1280]{1,0:T(2,128)(2,1)S(1)}, u32[]{:S(2)}, u32[]{:S(2)}) %collective-permute-start.9) | collective-permute-done | bytes 5152 | tf_op jit(solution)/shard_map/ppermute | solution.py:192
  497.4 6.9 %collective-permute-done.11 = bf16[2,1280]{1,0:T(2,128)(2,1)S(1)} collective-permute-done((bf16[2,1280]{1,0:T(2,128)(2,1)S(1)}, bf16[2,1280]{1,0:T(2,128)(2,1)S(1)}, u32[]{:S(2)}, u32[]{:S(2)}) %collective-permute-start.11) | collective-permute-done | bytes 5152 | tf_op jit(solution)/shard_map/ppermute | solution.py:192
  504.9 6.9 %collective-permute-done.12 = bf16[2,1280]{1,0:T(2,128)(2,1)S(1)} collective-permute-done((bf16[2,1280]{1,0:T(2,128)(2,1)S(1)}, bf16[2,1280]{1,0:T(2,128)(2,1)S(1)}, u32[]{:S(2)}, u32[]{:S(2)}) %collective-permute-start.12) | collective-permute-done | bytes 5152 | tf_op jit(solution)/shard_map/ppermute | solution.py:192
  512.4 7.0 %collective-permute-done.13 = bf16[2,1280]{1,0:T(2,128)(2,1)} collective-permute-done((bf16[2,1280]{1,0:T(2,128)(2,1)S(1)}, bf16[2,1280]{1,0:T(2,128)(2,1)}, u32[]{:S(2)}, u32[]{:S(2)}) %collective-permute-start.13) | collective-permute-done | bytes 5152 | tf_op jit(solution)/shard_map/ppermute | solution.py:192
  540.0 84.9 %all-reduce.3.cloned.1.call-done = bf16[32,1280]{1,0:T(8,128)(2,1)} async-done(((bf16[32,1280]{1,0:T(8,128)(2,1)}), bf16[32,1280]{1,0:T(8,128)(2,1)}) %all-reduce.3.cloned.1.call-update) | async-done | bytes 81936
  (130 shorter events, 71.8 us)
Async XLA Ops:
  11.9 35.5 %all-to-all-start = ((bf16[16,1,1]{2,1,0:T(2,128)(2,1)}), bf16[16,1,1]{2,1,0:T(2,128)(2,1)S(1)}, u32[]{:S(2)}, u32[]{:S(2)}) async-start(bf16[16,1,1]{2,1,0:T(2,128)(2,1)} %copy.91), calls=%async_computation | async-start | bytes 16384 | tf_op jit(solution)/shard_map/all_to_all | solution.py:99
  47.5 24.5 %all-to-all-start.1 = ((bf16[16,2,240]{2,1,0:T(2,128)(2,1)}), bf16[16,2,240]{2,1,0:T(2,128)(2,1)S(1)}, u32[]{:S(2)}, u32[]{:S(2)}) async-start(bf16[16,2,240]{2,1,0:T(2,128)(2,1)} %all_to_all.35), calls=%async_computation.1 | async-start | bytes 32768 | tf_op jit(solution)/shard_map/all_to_all | solution.py:31
  72.0 235.0 %all-to-all-start.2 = ((bf16[16,128,2560]{2,1,0:T(8,128)(2,1)}), bf16[16,128,2560]{2,1,0:T(8,128)(2,1)}, u32[]{:S(2)}, u32[]{:S(2)}) async-start(bf16[16,128,2560]{2,1,0:T(8,128)(2,1)} %copy.94), calls=%async_computation.2 | async-start | bytes 20971520 | tf_op jit(solution)/shard_map/all_to_all | solution.py:98
  79.3 545.5 %all-reduce.3.cloned.1.call-start = ((), (), s32[]{:S(2)}) async-start(), calls=%async_computation.4 | async-start | bytes 163840
  362.8 57.2 %copy-start.2 = (bf16[2,1280]{1,0:T(2,128)(2,1)S(1)}, bf16[2,1280]{1,0:T(2,128)(2,1)}, u32[]{:S(2)}) copy-start(bf16[2,1280]{1,0:T(2,128)(2,1)} %param.18) | copy-start | bytes 15364
  362.8 57.2 %copy-start.5 = (f32[1280]{0:T(1024)S(1)}, f32[1280]{0:T(1024)}, u32[]{:S(2)}) copy-start(f32[1280]{0:T(1024)} %param.32) | copy-start | bytes 15364
  362.8 170.6 %copy-start.1 = (bf16[1280,320]{0,1:T(8,128)(2,1)S(1)}, bf16[1280,320]{0,1:T(8,128)(2,1)}, u32[]{:S(2)}) copy-start(bf16[1280,320]{0,1:T(8,128)(2,1)} %param.29) | copy-start | bytes 2457604
  420.8 7.0 %collective-permute-start = (bf16[2,1280]{1,0:T(2,128)(2,1)S(1)}, bf16[2,1280]{1,0:T(2,128)(2,1)S(1)}, u32[]{:S(2)}, u32[]{:S(2)}) collective-permute-start(bf16[2,1280]{1,0:T(2,128)(2,1)S(1)} %multiply_convert_fusion.3), channel_id=1, source_target_pairs={{0,1},{1,2},{2,3},{3,4},{4,5},{5,6},{6,7},{7,8},{8,9},{9,10},{10,1... | collective-permute-start | bytes 15368 | tf_op jit(solution)/shard_map/ppermute | solution.py:192
  427.8 6.9 %collective-permute-start.1 = (bf16[2,1280]{1,0:T(2,128)(2,1)S(1)}, bf16[2,1280]{1,0:T(2,128)(2,1)S(1)}, u32[]{:S(2)}, u32[]{:S(2)}) collective-permute-start(bf16[2,1280]{1,0:T(2,128)(2,1)S(1)} %collective-permute-done), channel_id=1, source_target_pairs={{0,1},{1,2},{2,3},{3,4},{4,5},{5,6},{6,7},{7,8},{8,9},{9,10},{10,1... | collective-permute-start | bytes 15368 | tf_op jit(solution)/shard_map/ppermute | solution.py:192
  434.7 6.9 %collective-permute-start.2 = (bf16[2,1280]{1,0:T(2,128)(2,1)S(1)}, bf16[2,1280]{1,0:T(2,128)(2,1)S(1)}, u32[]{:S(2)}, u32[]{:S(2)}) collective-permute-start(bf16[2,1280]{1,0:T(2,128)(2,1)S(1)} %collective-permute-done.1), channel_id=1, source_target_pairs={{0,1},{1,2},{2,3},{3,4},{4,5},{5,6},{6,7},{7,8},{8,9},{9,10},{10,1... | collective-permute-start | bytes 15368 | tf_op jit(solution)/shard_map/ppermute | solution.py:192
  441.7 6.9 %collective-permute-start.3 = (bf16[2,1280]{1,0:T(2,128)(2,1)S(1)}, bf16[2,1280]{1,0:T(2,128)(2,1)S(1)}, u32[]{:S(2)}, u32[]{:S(2)}) collective-permute-start(bf16[2,1280]{1,0:T(2,128)(2,1)S(1)} %collective-permute-done.2), channel_id=1, source_target_pairs={{0,1},{1,2},{2,3},{3,4},{4,5},{5,6},{6,7},{7,8},{8,9},{9,10},{10,1... | collective-permute-start | bytes 15368 | tf_op jit(solution)/shard_map/ppermute | solution.py:192
  448.6 6.9 %collective-permute-start.4 = (bf16[2,1280]{1,0:T(2,128)(2,1)S(1)}, bf16[2,1280]{1,0:T(2,128)(2,1)S(1)}, u32[]{:S(2)}, u32[]{:S(2)}) collective-permute-start(bf16[2,1280]{1,0:T(2,128)(2,1)S(1)} %collective-permute-done.3), channel_id=1, source_target_pairs={{0,1},{1,2},{2,3},{3,4},{4,5},{5,6},{6,7},{7,8},{8,9},{9,10},{10,1... | collective-permute-start | bytes 15368 | tf_op jit(solution)/shard_map/ppermute | solution.py:192
  455.5 6.9 %collective-permute-start.5 = (bf16[2,1280]{1,0:T(2,128)(2,1)S(1)}, bf16[2,1280]{1,0:T(2,128)(2,1)S(1)}, u32[]{:S(2)}, u32[]{:S(2)}) collective-permute-start(bf16[2,1280]{1,0:T(2,128)(2,1)S(1)} %collective-permute-done.4), channel_id=1, source_target_pairs={{0,1},{1,2},{2,3},{3,4},{4,5},{5,6},{6,7},{7,8},{8,9},{9,10},{10,1... | collective-permute-start | bytes 15368 | tf_op jit(solution)/shard_map/ppermute | solution.py:192
  462.5 6.9 %collective-permute-start.6 = (bf16[2,1280]{1,0:T(2,128)(2,1)S(1)}, bf16[2,1280]{1,0:T(2,128)(2,1)S(1)}, u32[]{:S(2)}, u32[]{:S(2)}) collective-permute-start(bf16[2,1280]{1,0:T(2,128)(2,1)S(1)} %collective-permute-done.5), channel_id=1, source_target_pairs={{0,1},{1,2},{2,3},{3,4},{4,5},{5,6},{6,7},{7,8},{8,9},{9,10},{10,1... | collective-permute-start | bytes 15368 | tf_op jit(solution)/shard_map/ppermute | solution.py:192
  469.4 6.9 %collective-permute-start.7 = (bf16[2,1280]{1,0:T(2,128)(2,1)S(1)}, bf16[2,1280]{1,0:T(2,128)(2,1)S(1)}, u32[]{:S(2)}, u32[]{:S(2)}) collective-permute-start(bf16[2,1280]{1,0:T(2,128)(2,1)S(1)} %collective-permute-done.6), channel_id=1, source_target_pairs={{0,1},{1,2},{2,3},{3,4},{4,5},{5,6},{6,7},{7,8},{8,9},{9,10},{10,1... | collective-permute-start | bytes 15368 | tf_op jit(solution)/shard_map/ppermute | solution.py:192
  476.4 6.9 %collective-permute-start.8 = (bf16[2,1280]{1,0:T(2,128)(2,1)S(1)}, bf16[2,1280]{1,0:T(2,128)(2,1)S(1)}, u32[]{:S(2)}, u32[]{:S(2)}) collective-permute-start(bf16[2,1280]{1,0:T(2,128)(2,1)S(1)} %collective-permute-done.7), channel_id=1, source_target_pairs={{0,1},{1,2},{2,3},{3,4},{4,5},{5,6},{6,7},{7,8},{8,9},{9,10},{10,1... | collective-permute-start | bytes 15368 | tf_op jit(solution)/shard_map/ppermute | solution.py:192
  483.3 6.9 %collective-permute-start.9 = (bf16[2,1280]{1,0:T(2,128)(2,1)S(1)}, bf16[2,1280]{1,0:T(2,128)(2,1)S(1)}, u32[]{:S(2)}, u32[]{:S(2)}) collective-permute-start(bf16[2,1280]{1,0:T(2,128)(2,1)S(1)} %collective-permute-done.8), channel_id=1, source_target_pairs={{0,1},{1,2},{2,3},{3,4},{4,5},{5,6},{6,7},{7,8},{8,9},{9,10},{10,1... | collective-permute-start | bytes 15368 | tf_op jit(solution)/shard_map/ppermute | solution.py:192
  490.2 7.1 %collective-permute-start.10 = (bf16[2,1280]{1,0:T(2,128)(2,1)S(1)}, bf16[2,1280]{1,0:T(2,128)(2,1)S(1)}, u32[]{:S(2)}, u32[]{:S(2)}) collective-permute-start(bf16[2,1280]{1,0:T(2,128)(2,1)S(1)} %collective-permute-done.9), channel_id=1, source_target_pairs={{0,1},{1,2},{2,3},{3,4},{4,5},{5,6},{6,7},{7,8},{8,9},{9,10},{10,1... | collective-permute-start | bytes 15368 | tf_op jit(solution)/shard_map/ppermute | solution.py:192
  497.4 6.9 %collective-permute-start.11 = (bf16[2,1280]{1,0:T(2,128)(2,1)S(1)}, bf16[2,1280]{1,0:T(2,128)(2,1)S(1)}, u32[]{:S(2)}, u32[]{:S(2)}) collective-permute-start(bf16[2,1280]{1,0:T(2,128)(2,1)S(1)} %collective-permute-done.10), channel_id=1, source_target_pairs={{0,1},{1,2},{2,3},{3,4},{4,5},{5,6},{6,7},{7,8},{8,9},{9,10},{10,1... | collective-permute-start | bytes 15368 | tf_op jit(solution)/shard_map/ppermute | solution.py:192
  504.9 6.9 %collective-permute-start.12 = (bf16[2,1280]{1,0:T(2,128)(2,1)S(1)}, bf16[2,1280]{1,0:T(2,128)(2,1)S(1)}, u32[]{:S(2)}, u32[]{:S(2)}) collective-permute-start(bf16[2,1280]{1,0:T(2,128)(2,1)S(1)} %collective-permute-done.11), channel_id=1, source_target_pairs={{0,1},{1,2},{2,3},{3,4},{4,5},{5,6},{6,7},{7,8},{8,9},{9,10},{10,1... | collective-permute-start | bytes 15368 | tf_op jit(solution)/shard_map/ppermute | solution.py:192
  512.4 7.0 %collective-permute-start.13 = (bf16[2,1280]{1,0:T(2,128)(2,1)S(1)}, bf16[2,1280]{1,0:T(2,128)(2,1)}, u32[]{:S(2)}, u32[]{:S(2)}) collective-permute-start(bf16[2,1280]{1,0:T(2,128)(2,1)S(1)} %collective-permute-done.12), channel_id=1, source_target_pairs={{0,1},{1,2},{2,3},{3,4},{4,5},{5,6},{6,7},{7,8},{8,9},{9,10},{10,1... | collective-permute-start | bytes 15368 | tf_op jit(solution)/shard_map/ppermute | solution.py:192
  519.5 7.3 %collective-permute-start.14 = (bf16[2,1280]{1,0:T(2,128)(2,1)}, bf16[2,1280]{1,0:T(2,128)(2,1)}, u32[]{:S(2)}, u32[]{:S(2)}) collective-permute-start(bf16[2,1280]{1,0:T(2,128)(2,1)} %collective-permute-done.13), channel_id=1, source_target_pairs={{0,1},{1,2},{2,3},{3,4},{4,5},{5,6},{6,7},{7,8},{8,9},{9,10},{10,1... | collective-permute-start | bytes 15368 | tf_op jit(solution)/shard_map/ppermute | solution.py:192
  538.8 86.9 %copy-start.7 = (f32[1280]{0:T(1024)S(1)}, f32[1280]{0:T(1024)}, u32[]{:S(2)}) copy-start(f32[1280]{0:T(1024)} %param.33) | copy-start | bytes 15364
  538.8 86.9 %copy-start.9 = (f32[2]{0:T(128)S(1)}, f32[2]{0:T(128)}, u32[]{:S(2)}) copy-start(f32[2]{0:T(128)} %copy-done.8) | copy-start | bytes 28
  (7 other events, 61.5 us)
Sparse Core Ops, SparseCore 0:
  537.6 87.1 all-reduce.2
